TPU v7x, 32 devices: a whole 2x2x4 slice. The times are simulated.
32 devices in a mesh: row: 4 (over x, core), col: 8 (over z, y).
Axes of the slice: x: 2, y: 2, z: 4, core: 2. Of those that a mesh axis runs over, the one named last changes fastest.
Arguments:
- embeddings: bfloat16 [4096, 512], P(('row', 'col')), may hold values from -6 to 6
- sketch: bfloat16 [4096, 64], P(('row', 'col')), may hold values from -240 to 240
Outputs:
- basis: float32 [4096, 64], P(('row', 'col'))
- first_pass: float32 [4096, 64], P(('row', 'col'))
All inputs are finite; a program needn't handle non-finite values.
Results may differ from a plain program's by a relative error of at most 0.00205.
Values may be sent and summed in bfloat16 or wider, within the bound.
No kernel may reach another device: no remote copies, remote signals or barrier semaphores. Data moves between devices by JAX's collectives and lax.ppermute only.
A program may use at most 64 MiB of HBM per device.

v0:
```python
import jax
import jax.numpy as jnp
from jax import lax
from jax.sharding import PartitionSpec as P


def squares_of(points):
    return jnp.sum(jnp.square(points.astype(jnp.float32)), axis=1)


def kernel_tile(left, right, left_sq, right_sq, gamma):
    cross = lax.dot_general(
        left, right, (((1,), (1,)), ((), ())), preferred_element_type=jnp.float32
    )
    dist = left_sq[:, None] + right_sq[None, :] - 2.0 * cross
    return jnp.exp(-gamma * dist).astype(jnp.bfloat16)


def product_of(left, right):
    return lax.dot_general(
        left,
        right,
        (((0,), (0,)), ((), ())),
        precision=lax.Precision.HIGHEST,
        preferred_element_type=jnp.float32,
    )


def per_device(embeddings, sketch):
    width = embeddings.shape[1]
    gamma = 3.0 / width
    own_points = lax.all_gather(embeddings, "row", axis=0, tiled=True)
    own_sq = squares_of(own_points)
    empty = jnp.zeros((own_points.shape[0], sketch.shape[1]), jnp.float32)
    total = empty
    points = lax.all_gather(embeddings, "col", axis=0, tiled=True)
    tests = lax.all_gather(sketch, "col", axis=0, tiled=True)
    count = points.shape[0]
    size = 512

    def step(carry, block):
        block_points, block_tests = block
        tile = kernel_tile(own_points, block_points, own_sq, squares_of(block_points), gamma)
        return (carry + jnp.dot(tile, block_tests, preferred_element_type=jnp.float32), None)

    stacked = (
        points.reshape(count // size, size, width),
        tests.reshape(count // size, size, tests.shape[1]),
    )
    total, unused = lax.scan(step, total, stacked)
    sketched = lax.psum_scatter(total, "row", scatter_dimension=0, tiled=True)
    core = lax.psum(product_of(sketch.astype(jnp.float32), sketched), ("row", "col"))
    lower = jnp.linalg.cholesky(core)
    first = jax.scipy.linalg.solve_triangular(lower, sketched.T, lower=True).T
    gram_two = lax.psum(product_of(first, first), ("row", "col"))
    lower_two = jnp.linalg.cholesky(gram_two)
    second = jax.scipy.linalg.solve_triangular(lower_two, first.T, lower=True).T
    total_points = sketched.shape[0] * lax.axis_size("row") * lax.axis_size("col")
    scale = jnp.sqrt(jnp.float32(total_points))
    return (second * scale, first * scale)


def solution(mesh):
    placed = (P(("row", "col"), None), P(("row", "col"), None))
    return jax.shard_map(
        per_device,
        mesh=mesh,
        in_specs=placed,
        out_specs=(P(("row", "col"), None), P(("row", "col"), None)),
        check_vma=False,
    )
```

profile of v0, /device:TPU:0, one launch (start us, length us, event | category | flops | bytes accessed | tf_op | source)
XLA Modules:
  0.0 193.4 jit_solution(8559707278417701284)
XLA Ops:
  7.2 0.0 copy-start.3
  7.2 0.0 all-gather.2.cloned.1.call-start
  7.2 0.7 all-gather.2.cloned.1.call-update
  7.9 0.0 reduce-scatter.2.cloned.1.call-start
  8.0 0.0 copy-done.3
  8.0 28.2 %all_gather.11 = bf16[1024,64]{0,1:T(8,128)(2,1)S(1)} all-gather(bf16[128,64]{0,1:T(8,128)(2,1)S(1)} %copy-done.3), channel_id=1, replica_groups=mesh['row'=4,'col'=8] {'col'}, dimensions={0}, use_global_device_ids=true | all-gather | bytes 147456 | tf_op jit(solution)/shard_map/all_gather | solution.py:37
  36.2 0.0 copy-start
  36.2 0.2 copy.4
  36.4 0.7 copy-done
  37.1 7.2 %all_gather.9 = bf16[512,512]{1,0:T(8,128)(2,1)S(1)} all-gather(bf16[128,512]{1,0:T(8,128)(2,1)S(1)} %copy-done), channel_id=1, replica_groups=mesh['row'=4,'col'=8] {'row'}, dimensions={0}, use_global_device_ids=true | all-gather | bytes 655360 | tf_op jit(solution)/shard_map/all_gather | solution.py:32
  44.3 0.2 multiply_reduce_fusion.1
  44.5 9.1 %all-gather.2.cloned.1.call-done = bf16[1024,512]{1,0:T(8,128)(2,1)} async-done(((bf16[128,512]{1,0:T(8,128)(2,1)}), bf16[1024,512]{1,0:T(8,128)(2,1)}) %all-gather.2.cloned.1.call-update) | async-done | bytes 1048592 | tf_op jit(solution)/shard_map/all_gather | solution.py:36
  53.6 6.2 %while.11 = (s32[]{:T(128)}, f32[512,64]{0,1:T(8,128)S(1)}, f32[512]{0:T(512)S(1)}, bf16[2,512,512]{2,1,0:T(8,128)(2,1)}, bf16[512,512]{1,0:T(8,128)(2,1)S(1)}, ...) while((s32[]{:T(128)}, f32[512,64]{0,1:T(8,128)S(1)}, f32[512]{0:T(512)S(1)}, ...), condition=%wide.region_3.4_spmd.clone, body=%wide.region_1.3_spmd.clone.sunk | while | flops 304152064 | bytes 1973347 | solution.py:50
  53.6 1.2 multiply_reduce_fusion.3
  54.8 1.8 fusion.47
  56.6 1.2 multiply_reduce_fusion.3
  57.9 1.8 fusion.47
  59.7 0.0 copy-start.2
  59.7 0.6 copy-done.2
  60.4 0.0 reduce-scatter.2.cloned.1.call-update
  60.4 18.5 %reduce-scatter.2.cloned.1.call-done = f32[128,64]{0,1:T(8,128)} async-done(((f32[512,64]{0,1:T(8,128)}), f32[128,64]{0,1:T(8,128)}) %reduce-scatter.2.cloned.1.call-update) | async-done | bytes 32784 | tf_op jit(solution)/shard_map/reduce_scatter | solution.py:51
  78.9 0.9 convolution_bitcast_fusion
  79.8 39.4 %psum.14 = f32[64,64]{0,1:T(8,128)S(1)} all-reduce(f32[64,64]{0,1:T(8,128)S(1)} %convolution_bitcast_fusion), channel_id=1, replica_groups=mesh['row'=4,'col'=8] {'row','col'}, use_global_device_ids=true, to_apply=%region_5.6 | all-reduce | flops 4096 | bytes 32768 | tf_op jit(solution)/shard_map/psum | solution.py:52
  119.3 0.1 copy.5
  119.3 5.8 %cholesky.44 = f32[64,64]{1,0:T(8,128)S(1)} custom-call(f32[64,64]{1,0:T(8,128)S(1)} %fusion.30), custom_call_target="Cholesky" | custom-call | tf_op jit(solution)/shard_map/jit(cholesky)/cholesky | solution.py:53
  125.2 0.6 compare_reduce_fusion.1
  125.9 0.0 copy-start.1
  125.9 0.7 fusion.23
  126.5 4.9 %custom-call.7 = f32[1,64,64]{1,2,0:T(8,128)S(1)} custom-call(f32[1,64,64]{2,1,0:T(8,128)S(1)} %fusion.23), custom_call_target="InvertDiagBlocksLowerTriangular" | custom-call | tf_op jit(solution)/shard_map/jit(_solve_triangular)/triangular_solve | solution.py:54
  131.4 0.0 copy-done.1
  131.5 0.2 fusion.27
  131.7 0.2 fusion.33
  131.9 0.6 multiply_bitcast_fusion
  132.5 41.0 %psum.15 = f32[64,64]{0,1:T(8,128)S(1)} all-reduce(f32[64,64]{0,1:T(8,128)S(1)} %fusion.33), channel_id=1, replica_groups=mesh['row'=4,'col'=8] {'row','col'}, use_global_device_ids=true, to_apply=%region_8.11 | all-reduce | flops 4096 | bytes 32768 | tf_op jit(solution)/shard_map/psum | solution.py:55
  173.5 0.1 copy.7
  173.6 5.8 %cholesky.55 = f32[64,64]{1,0:T(8,128)S(1)} custom-call(f32[64,64]{1,0:T(8,128)S(1)} %fusion.26), custom_call_target="Cholesky" | custom-call | tf_op jit(solution)/shard_map/jit(cholesky)/cholesky | solution.py:56
  179.5 0.6 compare_reduce_fusion
  180.2 0.7 fusion.24
  180.8 4.9 %custom-call.8 = f32[1,64,64]{1,2,0:T(8,128)S(1)} custom-call(f32[1,64,64]{2,1,0:T(8,128)S(1)} %fusion.24), custom_call_target="InvertDiagBlocksLowerTriangular" | custom-call | tf_op jit(solution)/shard_map/jit(_solve_triangular)/triangular_solve | solution.py:57
  185.7 0.9 fusion.22
  (5 shorter events, 0.1 us)
Async XLA Ops:
  7.2 0.8 copy-start.3
  7.2 46.4 %all-gather.2.cloned.1.call-start = ((), (), s32[]{:S(2)}) async-start(), calls=%async_computation.1 | async-start | bytes 1179648 | tf_op jit(solution)/shard_map/all_gather | solution.py:36
  7.9 71.0 %reduce-scatter.2.cloned.1.call-start = ((), (), s32[]{:S(2)}) async-start(), calls=%async_computation.2 | async-start | bytes 163840 | tf_op jit(solution)/shard_map/reduce_scatter | solution.py:51
  36.2 0.9 copy-start
  59.7 0.6 copy-start.2
  125.9 5.6 %copy-start.1 = (f32[128,64]{0,1:T(8,128)S(1)}, f32[128,64]{0,1:T(8,128)}, u32[]{:S(2)}) copy-start(f32[128,64]{0,1:T(8,128)} %reduce-scatter.2.cloned.1.call-done) | copy-start | bytes 98308
Sparse Core Ops, SparseCore 0:
  10.1 43.4 all-gather.1
  60.5 18.3 reduce-scatter.1
where the time goes:
time: 194 us; the launch traced here: 193 us
  blocking collectives  116 us (60%)
  waiting for transfers between devices  28.3 us (15%)
  other arithmetic  27.4 us (14%)
  between operations  14.2 us (7%)
  matrix products  5.88 us (3%)
    psum x1, blocking collectives, per_device(): gram_two = lax.psum(product_of(first, first), ('row', 'col'))  41 us
    psum x1, blocking collectives, per_device(): lax.psum(product_of(sketch.astype(jnp.float32), sketched), ('row', 'col'))  39.4 us
    all_gather x1, blocking collectives, per_device(): tests = lax.all_gather(sketch, 'col', axis=0, tiled=True)  28.2 us
    reduce_scatter x1, waiting for transfers between devices, per_device(): sketched = lax.psum_scatter(total, 'row', scatter_dimension=0, tiled=True)  18.5 us
    all_gather x1, waiting for transfers between devices, per_device(): points = lax.all_gather(embeddings, 'col', axis=0, tiled=True)  9.11 us
    all_gather x1, blocking collectives, per_device(): own_points = lax.all_gather(embeddings, 'row', axis=0, tiled=True)  7.18 us
    another operation x3, other arithmetic, per_device(): lower_two = jnp.linalg.cholesky(gram_two)  6.52 us
    another operation x3, other arithmetic, per_device(): lower = jnp.linalg.cholesky(core)  6.52 us
  transfers between devices with their start and end apart: 2, of which 2 were waited for; matrix products, arithmetic and copies ran while one was open for 0% of the time, Pallas kernels for 0%

commit v1 on v0

--- a/solution.py
+++ b/solution.py
@@ -52,7 +52,7 @@
     core = lax.psum(product_of(sketch.astype(jnp.float32), sketched), ("row", "col"))
     lower = jnp.linalg.cholesky(core)
     first = jax.scipy.linalg.solve_triangular(lower, sketched.T, lower=True).T
-    gram_two = lax.psum(product_of(first, first), ("row", "col"))
+    gram_two = jnp.sum(lax.all_gather(product_of(first, first), ("row", "col")), axis=0)
     lower_two = jnp.linalg.cholesky(gram_two)
     second = jax.scipy.linalg.solve_triangular(lower_two, first.T, lower=True).T
     total_points = sketched.shape[0] * lax.axis_size("row") * lax.axis_size("col")

time: 194 us -> 226 us (1.16)
  blocking collectives: 116 us -> 148 us
    all_gather x0 -> x1, blocking collectives: none -> 73.1 us  [per_device(): lax.all_gather(product_of(first, first), ('row', 'col'))]
    psum x1 -> x0, blocking collectives: 41 us -> none  [per_device(): gram_two = lax.psum(product_of(first, first), ('row', 'col'))]
where the time goes in v1:
time: 226 us
  blocking collectives  148 us (65%)
  waiting for transfers between devices  28.3 us (13%)
  other arithmetic  27.5 us (12%)
  between operations  14.2 us (6%)
  matrix products  5.88 us (3%)
    all_gather x1, blocking collectives, per_device(): lax.all_gather(product_of(first, first), ('row', 'col'))  73.1 us
    psum x1, blocking collectives, per_device(): lax.psum(product_of(sketch.astype(jnp.float32), sketched), ('row', 'col'))  39.4 us
    all_gather x1, blocking collectives, per_device(): tests = lax.all_gather(sketch, 'col', axis=0, tiled=True)  28.2 us
    reduce_scatter x1, waiting for transfers between devices, per_device(): sketched = lax.psum_scatter(total, 'row', scatter_dimension=0, tiled=True)  18.5 us
    all_gather x1, waiting for transfers between devices, per_device(): points = lax.all_gather(embeddings, 'col', axis=0, tiled=True)  9.11 us
    all_gather x1, blocking collectives, per_device(): own_points = lax.all_gather(embeddings, 'row', axis=0, tiled=True)  7.18 us
    another operation x3, other arithmetic, per_device(): lower_two = jnp.linalg.cholesky(gram_two)  6.52 us
    another operation x3, other arithmetic, per_device(): lower = jnp.linalg.cholesky(core)  6.52 us
  transfers between devices with their start and end apart: 2, of which 2 were waited for; matrix products, arithmetic and copies ran while one was open for 0% of the time, Pallas kernels for 0%

profile of v1, /device:TPU:0, one launch (start us, length us, event | category | flops | bytes accessed | tf_op | source)
XLA Modules:
  0.0 225.6 jit_solution(6368206625257600249)
XLA Ops:
  7.2 0.0 copy-start.3
  7.2 0.0 all-gather.3.cloned.1.call-start
  7.2 0.7 all-gather.3.cloned.1.call-update
  7.9 0.0 reduce-scatter.2.cloned.1.call-start
  8.0 0.0 copy-done.3
  8.0 28.2 %all_gather.17 = bf16[1024,64]{0,1:T(8,128)(2,1)S(1)} all-gather(bf16[128,64]{0,1:T(8,128)(2,1)S(1)} %copy-done.3), channel_id=1, replica_groups=mesh['row'=4,'col'=8] {'col'}, dimensions={0}, use_global_device_ids=true | all-gather | bytes 147456 | tf_op jit(solution)/shard_map/all_gather | solution.py:37
  36.2 0.0 copy-start
  36.2 0.2 copy.7
  36.4 0.7 copy-done
  37.1 7.2 %all_gather.15 = bf16[512,512]{1,0:T(8,128)(2,1)S(1)} all-gather(bf16[128,512]{1,0:T(8,128)(2,1)S(1)} %copy-done), channel_id=1, replica_groups=mesh['row'=4,'col'=8] {'row'}, dimensions={0}, use_global_device_ids=true | all-gather | bytes 655360 | tf_op jit(solution)/shard_map/all_gather | solution.py:32
  44.3 0.2 multiply_reduce_fusion.1
  44.5 9.1 %all-gather.3.cloned.1.call-done = bf16[1024,512]{1,0:T(8,128)(2,1)} async-done(((bf16[128,512]{1,0:T(8,128)(2,1)}), bf16[1024,512]{1,0:T(8,128)(2,1)}) %all-gather.3.cloned.1.call-update) | async-done | bytes 1048592 | tf_op jit(solution)/shard_map/all_gather | solution.py:36
  53.6 6.2 %while.11 = (s32[]{:T(128)}, f32[512,64]{0,1:T(8,128)S(1)}, f32[512]{0:T(512)S(1)}, bf16[2,512,512]{2,1,0:T(8,128)(2,1)}, bf16[512,512]{1,0:T(8,128)(2,1)S(1)}, ...) while((s32[]{:T(128)}, f32[512,64]{0,1:T(8,128)S(1)}, f32[512]{0:T(512)S(1)}, ...), condition=%wide.region_3.4_spmd.clone, body=%wide.region_1.3_spmd.clone.sunk | while | flops 304152064 | bytes 1973347 | solution.py:50
  53.6 1.2 multiply_reduce_fusion.3
  54.8 1.8 fusion.47
  56.6 1.2 multiply_reduce_fusion.3
  57.9 1.8 fusion.47
  59.7 0.0 copy-start.2
  59.7 0.6 copy-done.2
  60.4 0.0 reduce-scatter.2.cloned.1.call-update
  60.4 18.5 %reduce-scatter.2.cloned.1.call-done = f32[128,64]{0,1:T(8,128)} async-done(((f32[512,64]{0,1:T(8,128)}), f32[128,64]{0,1:T(8,128)}) %reduce-scatter.2.cloned.1.call-update) | async-done | bytes 32784 | tf_op jit(solution)/shard_map/reduce_scatter | solution.py:51
  78.9 0.9 convolution_bitcast_fusion
  79.8 39.4 %psum.7 = f32[64,64]{0,1:T(8,128)S(1)} all-reduce(f32[64,64]{0,1:T(8,128)S(1)} %convolution_bitcast_fusion), channel_id=1, replica_groups=mesh['row'=4,'col'=8] {'row','col'}, use_global_device_ids=true, to_apply=%region_5.6 | all-reduce | flops 4096 | bytes 32768 | tf_op jit(solution)/shard_map/psum | solution.py:52
  119.3 0.1 copy.8
  119.3 5.8 %cholesky.44 = f32[64,64]{1,0:T(8,128)S(1)} custom-call(f32[64,64]{1,0:T(8,128)S(1)} %fusion.30), custom_call_target="Cholesky" | custom-call | tf_op jit(solution)/shard_map/jit(cholesky)/cholesky | solution.py:53
  125.2 0.6 compare_reduce_fusion.1
  125.9 0.0 copy-start.1
  125.9 0.7 fusion.23
  126.5 4.9 %custom-call.7 = f32[1,64,64]{1,2,0:T(8,128)S(1)} custom-call(f32[1,64,64]{2,1,0:T(8,128)S(1)} %fusion.23), custom_call_target="InvertDiagBlocksLowerTriangular" | custom-call | tf_op jit(solution)/shard_map/jit(_solve_triangular)/triangular_solve | solution.py:54
  131.4 0.0 copy-done.1
  131.5 0.2 fusion.27
  131.7 0.2 fusion.33
  131.9 0.6 multiply_bitcast_fusion
  132.5 73.1 %all-gather = f32[2048,64]{1,0:T(8,128)S(1)} all-gather(f32[64,64]{1,0:T(8,128)S(1)} %fusion.33), channel_id=2, replica_groups=mesh['row'=4,'col'=8] {'row','col'}, dimensions={0}, use_global_device_ids=true | all-gather | bytes 540672 | tf_op jit(solution)/shard_map/all_gather | solution.py:55
  205.6 0.1 reduce_sum.28
  205.7 0.1 copy.9
  205.8 5.8 %cholesky.55 = f32[64,64]{1,0:T(8,128)S(1)} custom-call(f32[64,64]{1,0:T(8,128)S(1)} %fusion.26), custom_call_target="Cholesky" | custom-call | tf_op jit(solution)/shard_map/jit(cholesky)/cholesky | solution.py:56
  211.6 0.6 compare_reduce_fusion
  212.3 0.7 fusion.24
  212.9 4.9 %custom-call.8 = f32[1,64,64]{1,2,0:T(8,128)S(1)} custom-call(f32[1,64,64]{2,1,0:T(8,128)S(1)} %fusion.24), custom_call_target="InvertDiagBlocksLowerTriangular" | custom-call | tf_op jit(solution)/shard_map/jit(_solve_triangular)/triangular_solve | solution.py:57
  217.8 0.9 fusion.22
  (5 shorter events, 0.1 us)
Async XLA Ops:
  7.2 0.8 copy-start.3
  7.2 46.4 %all-gather.3.cloned.1.call-start = ((), (), s32[]{:S(2)}) async-start(), calls=%async_computation.1 | async-start | bytes 1179648 | tf_op jit(solution)/shard_map/all_gather | solution.py:36
  7.9 71.0 %reduce-scatter.2.cloned.1.call-start = ((), (), s32[]{:S(2)}) async-start(), calls=%async_computation.2 | async-start | bytes 163840 | tf_op jit(solution)/shard_map/reduce_scatter | solution.py:51
  36.2 0.9 copy-start
  59.7 0.6 copy-start.2
  125.9 5.6 %copy-start.1 = (f32[128,64]{0,1:T(8,128)S(1)}, f32[128,64]{0,1:T(8,128)}, u32[]{:S(2)}) copy-start(f32[128,64]{0,1:T(8,128)} %reduce-scatter.2.cloned.1.call-done) | copy-start | bytes 98308
Sparse Core Ops, SparseCore 0:
  10.1 43.4 all-gather.2
  60.5 18.3 reduce-scatter.1
